TPU v7x, 128 devices: a whole 4x4x4 slice. The times are simulated.
128 devices in a mesh: fit: 16 (over z, x), basis: 4 (over y_hi, core), occ: 2 (over y_lo).
Axes of the slice: x: 4, y: 4 (y_hi: 2, y_lo: 2; y = y_hi * 2 + y_lo), z: 4, core: 2. Of those that a mesh axis runs over, the one named last changes fastest.
Arguments:
- ints: bfloat16 [256, 12288, 128], P('fit', 'basis'), may hold values from -0.5 to 0.5
- coeffs: bfloat16 [12288, 128], P('fit', 'occ'), may hold values from -0.59765625 to 0.59765625
- offsets: int32 [192, 2], P('basis'), may hold values from 0 to 191
- mask: int32 [192, 2], P('basis'), may hold values 0 or 1
Outputs:
- exchange: float32 [12288, 4, 512], P(('fit', 'occ'), None, 'basis')
All inputs are finite; a program needn't handle non-finite values. No bound on the sum of `mask` on one device may be relied on, other than what follows from the above.
Results may differ from a plain program's by a relative error of at most 0.003.
Values may be sent and summed in bfloat16 or wider, within the bound.
A program may use at most 192 MiB of HBM per device.

v0:
```python
import jax
import jax.numpy as jnp
import numpy as np
from jax import lax
from jax.sharding import PartitionSpec as P

BLK = 64
NNZ = 2
MU_DEV = 128
SIGN_ENTRIES = (
    (0, 0, 0, 1),
    (0, 1, 1, 1),
    (0, 2, 2, 1),
    (0, 3, 3, 1),
    (1, 0, 1, -1),
    (1, 1, 0, 1),
    (1, 2, 3, -1),
    (1, 3, 2, 1),
    (2, 0, 2, -1),
    (2, 1, 3, 1),
    (2, 2, 0, 1),
    (2, 3, 1, -1),
    (3, 0, 3, -1),
    (3, 1, 2, -1),
    (3, 2, 1, 1),
    (3, 3, 0, 1),
)


def joined_along(parts, dim):
    parts = jnp.moveaxis(parts, 0, dim)
    shape = parts.shape
    return parts.reshape(*shape[:dim], shape[dim] * shape[dim + 1], *shape[dim + 2 :])


def from_everyone(shard, axis):
    size = lax.axis_size(axis)
    return lax.all_to_all(
        jnp.broadcast_to(shard[None], (size, *shard.shape)), axis, 0, 0, tiled=True
    )


def collect(shard, axis, dim):
    return joined_along(from_everyone(shard, axis), dim)


def split_up(shard, dim, size):
    shape = shard.shape
    parts = shard.reshape(*shape[:dim], size, shape[dim] // size, *shape[dim + 1 :])
    return jnp.moveaxis(parts, dim, 0)


def sum_at_owner(shard, axis, dim):
    parts = split_up(shard, dim, lax.axis_size(axis))
    arrived = lax.all_to_all(parts, axis, split_axis=0, concat_axis=0, tiled=True)
    return arrived.sum(axis=0)


def sign_table():
    table = np.zeros((4, 4, 4), np.float32)
    for entry in SIGN_ENTRIES:
        table[entry[0], entry[1], entry[2]] = entry[3]
    return table


def contract(rows_part, mixed):
    return lax.dot_general(
        rows_part, mixed, (((1,), (1,)), ((), ())), preferred_element_type=jnp.float32
    )


def shards(ints, coeffs, offsets, mask):
    full = collect(coeffs, "fit", 0)
    width = full.shape[1]
    blocks = full.reshape(-1, BLK, width)
    picked = jnp.take(blocks, offsets, axis=0) * mask[:, :, None, None].astype(jnp.bfloat16)
    picked = picked.reshape(offsets.shape[0], NNZ * BLK, width)
    aux_count, rows, stored = ints.shape
    grouped = ints.reshape(aux_count, rows // BLK, BLK, stored)
    half = jnp.einsum("arjk,rkw->rjaw", grouped, picked, preferred_element_type=jnp.float32)
    half = half.reshape(rows, aux_count * width).astype(jnp.bfloat16)
    window = half[:MU_DEV].astype(jnp.float32).reshape(MU_DEV, -1, 4)
    mixed = jnp.einsum("rqs,mkq->rmks", jnp.asarray(sign_table(), jnp.float32), window)
    mixed = mixed.reshape(4 * MU_DEV, -1).astype(jnp.bfloat16)
    terms = contract(lax.all_gather(half, "basis", axis=0, tiled=True), mixed)
    partial_fit = lax.psum_scatter(terms, "fit", scatter_dimension=0, tiled=True)
    result = sum_at_owner(partial_fit, "occ", 0)
    return result.reshape(result.shape[0], 4, MU_DEV)


def solution(mesh):
    return jax.shard_map(
        shards,
        mesh=mesh,
        in_specs=(P("fit", "basis", None), P("fit", "occ"), P("basis", None), P("basis", None)),
        out_specs=P(("fit", "occ"), None, "basis"),
        check_vma=False,
    )
```

profile of v0, /device:TPU:0, one launch (start us, length us, event | category | flops | bytes accessed | tf_op | source)
XLA Modules:
  0.0 463.8 jit_solution(10026369443056584956)
XLA Ops:
  6.5 2.2 broadcast_in_dim.26
  8.7 8.0 %all-to-all-start = ((bf16[16,768,64]{1,2,0:T(8,128)(2,1)}), bf16[16,768,64]{1,2,0:T(8,128)(2,1)}, u32[]{:S(2)}, u32[]{:S(2)}) async-start(bf16[16,768,64]{1,2,0:T(8,128)(2,1)} %broadcast_in_dim.26), calls=%async_computation | async-start | bytes 3145728 | tf_op jit(solution)/shard_map/all_to_all | solution.py:38
  16.8 0.7 convert_element_type.23
  17.8 0.7 compare_and_fusion
  18.6 0.7 compare_select_fusion
  19.5 21.8 %all-to-all-done = bf16[16,768,64]{1,2,0:T(8,128)(2,1)} async-done(((bf16[16,768,64]{1,2,0:T(8,128)(2,1)}), bf16[16,768,64]{1,2,0:T(8,128)(2,1)}, u32[]{:S(2)}, u32[]{:S(2)}) %all-to-all-start) | async-done | bytes 1572896 | tf_op jit(solution)/shard_map/all_to_all | solution.py:38
  41.4 3.1 copy.33
  44.4 2.0 gather_fusion
  46.4 1.8 copy.45
  48.3 17.7 %convert_bitcast_fusion = bf16[48,64,16,64]{1,3,2,0:T(8,128)(2,1)} fusion(bf16[16,48,64,128]{3,2,1,0:T(8,128)(2,1)} %bitcast.27, bf16[48,128,64,1]{1,0,2,3:T(8,128)(2,1)S(1)} %multiply_bitcast_fusion), kind=kOutput, calls=%fused_computation.3 | convolution fusion | flops 808452096 | bytes 19660800 | tf_op jit(solution)/shard_map/arjk,rkw->rjaw/dot_general | solution.py:80
  66.0 17.5 %copy.39 = bf16[48,64,16,64]{3,2,1,0:T(8,128)(2,1)} copy(bf16[48,64,16,64]{1,3,2,0:T(8,128)(2,1)} %convert_bitcast_fusion) | data formatting | bytes 12582912 | tf_op jit(solution)/shard_map/convert_element_type | solution.py:81
  83.6 17.3 %convert_element_type.26 = bf16[3072,1024]{1,0:T(8,128)(2,1)} reshape(bf16[48,64,16,64]{3,2,1,0:T(8,128)(2,1)} %copy.39) | data formatting | bytes 12582912 | tf_op jit(solution)/shard_map/convert_element_type | solution.py:81
  100.9 0.2 reduce-scatter.2.cloned.1.call-start
  101.1 0.5 copy.40
  101.7 0.2 reshape.31
  101.9 0.2 copy.44
  102.2 0.7 fusion.4
  102.8 1.8 copy.42
  104.7 152.5 %all-gather.2.cloned.1.call-done = bf16[12288,1024]{1,0:T(8,128)(2,1)} async-done(((bf16[3072,1024]{1,0:T(8,128)(2,1)}), bf16[12288,1024]{1,0:T(8,128)(2,1)}) %all-gather.2.cloned.1.call-update) | async-done | bytes 25165840 | tf_op jit(solution)/shard_map/all_gather | solution.py:85
  257.2 22.5 %fusion.5 = f32[12288,512]{1,0:T(8,128)} fusion(bf16[12288,1024]{1,0:T(8,128)(2,1)} %all-gather.2.cloned.1.call-done, bf16[128,8,4,128]{3,2,1,0:T(4,128)(2,1)S(1)} %bitcast.32), kind=kOutput, calls=%fused_computation.6 | convolution fusion | flops 12884901888 | bytes 51380224 | tf_op jit(solution)/shard_map/dot_general | solution.py:67
  279.7 152.8 %reduce-scatter.2.cloned.1.call-done = f32[768,512]{1,0:T(8,128)} async-done(((f32[12288,512]{1,0:T(8,128)}), f32[768,512]{1,0:T(8,128)}) %reduce-scatter.2.cloned.1.call-update) | async-done | bytes 1572880 | tf_op jit(solution)/shard_map/reduce_scatter | solution.py:86
  432.5 23.1 %all_to_all.10 = f32[2,384,512]{2,1,0:T(8,128)S(1)} all-to-all(f32[2,384,512]{2,1,0:T(8,128)} %bitcast.30), channel_id=1, replica_groups=mesh['fit'=16,'basis'=4,'occ'=2] {'occ'}, dimensions={0} | all-to-all | bytes 3145728 | tf_op jit(solution)/shard_map/all_to_all | solution.py:55
  455.6 0.2 reduce_sum.9
  455.8 1.1 reshape.33
  (16 shorter events, 0.8 us)
Async XLA Ops:
  8.7 32.6 %all-to-all-start = ((bf16[16,768,64]{1,2,0:T(8,128)(2,1)}), bf16[16,768,64]{1,2,0:T(8,128)(2,1)}, u32[]{:S(2)}, u32[]{:S(2)}) async-start(bf16[16,768,64]{1,2,0:T(8,128)(2,1)} %broadcast_in_dim.26), calls=%async_computation | async-start | bytes 3145728 | tf_op jit(solution)/shard_map/all_to_all | solution.py:38
  16.8 240.4 %all-gather.2.cloned.1.call-start = ((), (), s32[]{:S(2)}) async-start(), calls=%async_computation.3 | async-start | bytes 31457280 | tf_op jit(solution)/shard_map/all_gather | solution.py:85
  83.6 17.5 %slice-start = ((bf16[48,64,16,64]{1,3,2,0:T(8,128)(2,1)}), bf16[2,64,16,64]{1,3,2,0:T(8,128)(2,1)S(1)}, s32[]{:S(2)}) async-start(bf16[48,64,16,64]{1,3,2,0:T(8,128)(2,1)} %convert_bitcast_fusion), calls=%async_computation.5 | async-start | bytes 1048576 | tf_op jit(solution)/shard_map/slice | solution.py:82
  83.6 18.6 %copy-start = (bf16[4,4,4,1]{1,2,0,3:T(4,128)(2,1)S(1)}, bf16[4,4,4,1]{1,2,0,3:T(4,128)(2,1)}, u32[]{:S(2)}) copy-start(bf16[4,4,4,1]{1,2,0,3:T(4,128)(2,1)} %constant.32) | copy-start | bytes 388
  100.9 331.6 %reduce-scatter.2.cloned.1.call-start = ((), (), s32[]{:S(2)}) async-start(), calls=%async_computation.4 | async-start | bytes 26738688 | tf_op jit(solution)/shard_map/reduce_scatter | solution.py:86
Sparse Core Ops, SparseCore 0:
  101.0 156.1 all-gather.1
  279.8 152.6 reduce-scatter.1
where the time goes:
time: 465 us; the launch traced here: 464 us
  waiting for transfers between devices  327 us (70%)
  local copies, waits for them, and re-layouts  48.5 us (10%)
  matrix products  40.9 us (9%)
  blocking collectives  23.1 us (5%)
  between operations  13.5 us (3%)
  starting transfers between devices  8.3 us (2%)
    reduce_scatter x1, waiting for transfers between devices, shards(): lax.psum_scatter(terms, 'fit', scatter_dimension=0, tiled=True)  153 us
    all_gather x1, waiting for transfers between devices, shards(): terms = contract(lax.all_gather(half, 'basis', axis=0, tiled=True), mixed)  153 us
    convert_element_type x2, local copies, waits for them, and re-layouts, shards(): half = half.reshape(rows, aux_count * width).astype(jnp.bfloat16)  34.8 us
    all_to_all x1, blocking collectives, sum_at_owner(): lax.all_to_all(parts, axis, split_axis=0, concat_axis=0, tiled=True)  23.1 us
    dot_general x1, matrix products, contract(): lax.dot_general(rows_part, mixed, (((1,), (1,)), ((), ())), preferred_ele...  22.5 us
    all_to_all x1, waiting for transfers between devices, from_everyone(): lax.all_to_all(jnp.broadcast_to(shard[None], (size, *shard.shape)), axis,...  21.8 us
    dot_general x1, matrix products, shards(): jnp.einsum('arjk,rkw->rjaw', grouped, picked, preferred_element_type=jnp....  17.7 us
  transfers between devices with their start and end apart: 3, of which 3 were waited for; matrix products, arithmetic and copies ran while one was open for 1% of the time, Pallas kernels for 0%

commit v1 on v0

--- a/solution.py
+++ b/solution.py
@@ -25,6 +25,18 @@
     (3, 2, 1, 1),
     (3, 3, 0, 1),
 )
+
+
+def check_layers_all_up(vals):
+    return jnp.concatenate(
+        lax.all_to_all(
+            jnp.stack([vals] * lax.axis_size("basis"), axis=0),
+            axis_name="basis",
+            split_axis=0,
+            concat_axis=0,
+        ),
+        axis=0,
+    )
 
 
 def joined_along(parts, dim):
@@ -82,7 +94,7 @@
     window = half[:MU_DEV].astype(jnp.float32).reshape(MU_DEV, -1, 4)
     mixed = jnp.einsum("rqs,mkq->rmks", jnp.asarray(sign_table(), jnp.float32), window)
     mixed = mixed.reshape(4 * MU_DEV, -1).astype(jnp.bfloat16)
-    terms = contract(lax.all_gather(half, "basis", axis=0, tiled=True), mixed)
+    terms = contract(check_layers_all_up(half), mixed)
     partial_fit = lax.psum_scatter(terms, "fit", scatter_dimension=0, tiled=True)
     result = sum_at_owner(partial_fit, "occ", 0)
     return result.reshape(result.shape[0], 4, MU_DEV)

time: 465 us -> 599 us (1.29)
  waiting for transfers between devices: 327 us -> 442 us
  local copies, waits for them, and re-layouts: 48.5 us -> 59.1 us
  starting transfers between devices: 8.3 us -> 16.8 us
    all_to_all x0 -> x1, waiting for transfers between devices: none -> 271 us  [check_layers_all_up(): lax.all_to_all(jnp.stack([vals] * lax.axis_size('basis'), axis=0), axis_n...]
    all_gather x1 -> x0, waiting for transfers between devices: 153 us -> none  [shards(): terms = contract(lax.all_gather(half, 'basis', axis=0, tiled=True), mixed)]
    another operation x0 -> x1, local copies, waits for them, and re-layouts: none -> 10.8 us  [check_layers_all_up(): jnp.stack([vals] * lax.axis_size('basis'), axis=0)]
    all_to_all x0 -> x1, starting transfers between devices: none -> 8.55 us  [check_layers_all_up(): lax.all_to_all(jnp.stack([vals] * lax.axis_size('basis'), axis=0), axis_n...]
where the time goes in v1:
time: 599 us; the launch traced here: 597 us
  waiting for transfers between devices  442 us (74%)
  local copies, waits for them, and re-layouts  59.1 us (10%)
  matrix products  40.8 us (7%)
  blocking collectives  23.1 us (4%)
  starting transfers between devices  16.8 us (3%)
  between operations  13.5 us (2%)
    all_to_all x1, waiting for transfers between devices, check_layers_all_up(): lax.all_to_all(jnp.stack([vals] * lax.axis_size('basis'), axis=0), axis_n...  271 us
    reduce_scatter x1, waiting for transfers between devices, shards(): lax.psum_scatter(terms, 'fit', scatter_dimension=0, tiled=True)  149 us
    convert_element_type x2, local copies, waits for them, and re-layouts, shards(): half = half.reshape(rows, aux_count * width).astype(jnp.bfloat16)  34.7 us
    all_to_all x1, blocking collectives, sum_at_owner(): lax.all_to_all(parts, axis, split_axis=0, concat_axis=0, tiled=True)  23.1 us
    dot_general x1, matrix products, contract(): lax.dot_general(rows_part, mixed, (((1,), (1,)), ((), ())), preferred_ele...  22.5 us
    all_to_all x1, waiting for transfers between devices, from_everyone(): lax.all_to_all(jnp.broadcast_to(shard[None], (size, *shard.shape)), axis,...  21.9 us
    dot_general x1, matrix products, shards(): jnp.einsum('arjk,rkw->rjaw', grouped, picked, preferred_element_type=jnp....  17.6 us
  transfers between devices with their start and end apart: 3, of which 3 were waited for; matrix products, arithmetic and copies ran while one was open for 1% of the time, Pallas kernels for 0%

profile of v1, /device:TPU:0, one launch (start us, length us, event | category | flops | bytes accessed | tf_op | source)
XLA Modules:
  0.0 597.2 jit_solution(4700280571773173741)
XLA Ops:
  6.5 2.2 broadcast_in_dim.26
  8.7 8.0 %all-to-all-start = ((bf16[16,768,64]{1,2,0:T(8,128)(2,1)}), bf16[16,768,64]{1,2,0:T(8,128)(2,1)}, u32[]{:S(2)}, u32[]{:S(2)}) async-start(bf16[16,768,64]{1,2,0:T(8,128)(2,1)} %broadcast_in_dim.26), calls=%async_computation | async-start | bytes 3145728 | tf_op jit(solution)/shard_map/all_to_all | solution.py:50
  16.8 0.7 convert_element_type.25
  17.8 0.7 compare_and_fusion
  18.6 0.7 compare_select_fusion
  19.5 21.9 %all-to-all-done = bf16[16,768,64]{1,2,0:T(8,128)(2,1)} async-done(((bf16[16,768,64]{1,2,0:T(8,128)(2,1)}), bf16[16,768,64]{1,2,0:T(8,128)(2,1)}, u32[]{:S(2)}, u32[]{:S(2)}) %all-to-all-start) | async-done | bytes 1572896 | tf_op jit(solution)/shard_map/all_to_all | solution.py:50
  41.4 3.1 copy.33
  44.4 2.0 gather_fusion
  46.4 1.8 copy.45
  48.3 17.6 %convert_bitcast_fusion = bf16[48,64,16,64]{1,3,2,0:T(8,128)(2,1)} fusion(bf16[16,48,64,128]{3,2,1,0:T(8,128)(2,1)} %bitcast.28, bf16[48,128,64,1]{1,0,2,3:T(8,128)(2,1)S(1)} %multiply_bitcast_fusion), kind=kOutput, calls=%fused_computation.3 | convolution fusion | flops 808452096 | bytes 19660800 | tf_op jit(solution)/shard_map/arjk,rkw->rjaw/dot_general | solution.py:92
  65.9 17.5 %copy.39 = bf16[48,64,16,64]{3,2,1,0:T(8,128)(2,1)} copy(bf16[48,64,16,64]{1,3,2,0:T(8,128)(2,1)} %convert_bitcast_fusion) | data formatting | bytes 12582912 | tf_op jit(solution)/shard_map/convert_element_type | solution.py:93
  83.4 17.2 %convert_element_type.28 = bf16[3072,1024]{1,0:T(8,128)(2,1)} reshape(bf16[48,64,16,64]{3,2,1,0:T(8,128)(2,1)} %copy.39) | data formatting | bytes 12582912 | tf_op jit(solution)/shard_map/convert_element_type | solution.py:93
  100.7 10.8 %stack.2 = bf16[4,3072,1024]{2,1,0:T(8,128)(2,1)} broadcast(bf16[3072,1024]{1,0:T(8,128)(2,1)} %convert_element_type.28), dimensions={1,2} | broadcast | bytes 31457280 | tf_op jit(solution)/shard_map/stack | solution.py:33
  111.4 8.5 %all-to-all-start.1 = ((bf16[4,3072,1024]{2,1,0:T(8,128)(2,1)}), bf16[4,3072,1024]{2,1,0:T(8,128)(2,1)}, u32[]{:S(2)}, u32[]{:S(2)}) async-start(bf16[4,3072,1024]{2,1,0:T(8,128)(2,1)} %stack.2), calls=%async_computation.1 | async-start | bytes 50331648 | tf_op jit(solution)/shard_map/all_to_all | solution.py:32
  120.2 0.5 copy.40
  120.8 0.2 reshape.38
  121.0 0.2 copy.44
  121.2 0.7 fusion.4
  121.9 1.8 copy.42
  123.8 270.6 %all-to-all-done.1 = bf16[4,3072,1024]{2,1,0:T(8,128)(2,1)} async-done(((bf16[4,3072,1024]{2,1,0:T(8,128)(2,1)}), bf16[4,3072,1024]{2,1,0:T(8,128)(2,1)}, u32[]{:S(2)}, u32[]{:S(2)}) %all-to-all-start.1) | async-done | bytes 25165856 | tf_op jit(solution)/shard_map/all_to_all | solution.py:32
  394.4 22.5 %fusion.5 = f32[12288,512]{1,0:T(8,128)} fusion(bf16[12288,1024]{1,0:T(8,128)(2,1)} %bitcast.6, bf16[128,8,4,128]{3,2,1,0:T(4,128)(2,1)S(1)} %bitcast.33), kind=kOutput, calls=%fused_computation.6 | convolution fusion | flops 12884901888 | bytes 51380224 | tf_op jit(solution)/shard_map/dot_general | solution.py:79
  416.9 149.1 %reduce-scatter.2.cloned.1.call-done = f32[768,512]{1,0:T(8,128)} async-done(((f32[12288,512]{1,0:T(8,128)}), f32[768,512]{1,0:T(8,128)}) %reduce-scatter.2.cloned.1.call-update) | async-done | bytes 1572880 | tf_op jit(solution)/shard_map/reduce_scatter | solution.py:98
  566.0 23.1 %all_to_all.15 = f32[2,384,512]{2,1,0:T(8,128)S(1)} all-to-all(f32[2,384,512]{2,1,0:T(8,128)} %bitcast.31), channel_id=1, replica_groups=mesh['fit'=16,'basis'=4,'occ'=2] {'occ'}, dimensions={0} | all-to-all | bytes 3145728 | tf_op jit(solution)/shard_map/all_to_all | solution.py:67
  589.2 1.1 reshape.40
  (16 shorter events, 1.1 us)
Async XLA Ops:
  8.7 32.6 %all-to-all-start = ((bf16[16,768,64]{1,2,0:T(8,128)(2,1)}), bf16[16,768,64]{1,2,0:T(8,128)(2,1)}, u32[]{:S(2)}, u32[]{:S(2)}) async-start(bf16[16,768,64]{1,2,0:T(8,128)(2,1)} %broadcast_in_dim.26), calls=%async_computation | async-start | bytes 3145728 | tf_op jit(solution)/shard_map/all_to_all | solution.py:50
  111.4 8.8 %slice-start = ((bf16[48,64,16,64]{1,3,2,0:T(8,128)(2,1)}), bf16[2,64,16,64]{1,3,2,0:T(8,128)(2,1)S(1)}, s32[]{:S(2)}) async-start(bf16[48,64,16,64]{1,3,2,0:T(8,128)(2,1)} %convert_bitcast_fusion), calls=%async_computation.5 | async-start | bytes 1048576 | tf_op jit(solution)/shard_map/slice | solution.py:94
  111.4 9.8 %copy-start = (bf16[4,4,4,1]{1,2,0,3:T(4,128)(2,1)S(1)}, bf16[4,4,4,1]{1,2,0,3:T(4,128)(2,1)}, u32[]{:S(2)}) copy-start(bf16[4,4,4,1]{1,2,0,3:T(4,128)(2,1)} %constant.32) | copy-start | bytes 388
  111.4 283.0 %all-to-all-start.1 = ((bf16[4,3072,1024]{2,1,0:T(8,128)(2,1)}), bf16[4,3072,1024]{2,1,0:T(8,128)(2,1)}, u32[]{:S(2)}, u32[]{:S(2)}) async-start(bf16[4,3072,1024]{2,1,0:T(8,128)(2,1)} %stack.2), calls=%async_computation.1 | async-start | bytes 50331648 | tf_op jit(solution)/shard_map/all_to_all | solution.py:32
  120.0 446.0 %reduce-scatter.2.cloned.1.call-start = ((), (), s32[]{:S(2)}) async-start(), calls=%async_computation.4 | async-start | bytes 26738688 | tf_op jit(solution)/shard_map/reduce_scatter | solution.py:98
Sparse Core Ops, SparseCore 0:
  417.0 148.9 reduce-scatter.1
